TPU v7x, 32 devices: a whole 2x2x4 slice. The times are simulated.
32 devices in a mesh: grp: 4 (over y, x), tp: 8 (over z, core).
Axes of the slice: x: 2, y: 2, z: 4, core: 2. Of those that a mesh axis runs over, the one named last changes fastest.
Arguments:
- batch_sizes: int32 [4], P('grp'), may hold values from 1 to 16
- seq_lens: int32 [4, 16], P('grp'), may hold values from 1 to 2048
- page_table: int32 [4, 16, 128], P('grp', None, 'tp'), may hold values from 0 to 255, as said below
- queries: bfloat16 [4, 16, 4096], P('grp', None, 'tp'), may hold values from -4 to 14
- kv_pool: bfloat16 [4, 2048, 16, 1024], P('grp', 'tp'), may hold values from -7 to 7
- new_kv: bfloat16 [4, 16, 1024], P('grp'), may hold values from -6 to 6
- out_weight: bfloat16 [4096, 2880], P('tp', 'grp'), may hold values from -0.375 to 0.375
Outputs:
- mixed: float32 [4, 16, 2880], P('grp')
Inputs may be any that keep to these rules, and one draw needn't show every extreme that they name: `batch_sizes`: slots below a group's batch size are live; the others are empty and their outputs are zero. `seq_lens`: entries of empty slots are drawn but unused. `page_table`: for every group g and every t, the entries [g, :, t * 16 to (t + 1) * 16 - 1] are a permutation of 0 to 255.
All inputs are finite; a program needn't handle non-finite values.
Results may differ from a plain program's by a relative error of at most 0.007.
Values may be sent and summed in bfloat16 or wider, within the bound.
A program may use at most 64 MiB of HBM per device.

v0:
```python
import jax
import jax.numpy as jnp
from jax import lax
from jax.sharding import PartitionSpec as P

HEADS = 64
KV_HEADS = 8
HD = 64
SLOT_BLOCK = 2
PRECISE = lax.Precision.HIGHEST
NEG_BIG = -1e30


def attend_slots(query_rows, page_blocks, lengths, tp_index, tp_count, kv_heads):
    slot_count, page_count, page_len, row_width = page_blocks.shape
    head_dim = row_width // (2 * kv_heads)
    head_count = query_rows.shape[1] // head_dim
    group_size = head_count // kv_heads
    token_count = page_count * page_len
    token_rows = page_blocks.reshape(slot_count, token_count, row_width)
    key_rows = token_rows[:, :, : row_width // 2].reshape(
        slot_count, token_count, kv_heads, head_dim
    )
    value_rows = token_rows[:, :, row_width // 2 :].reshape(
        slot_count, token_count, kv_heads, head_dim
    )
    grouped = query_rows.reshape(slot_count, kv_heads, group_size, head_dim)
    scores = jnp.einsum("skgd,stkd->skgt", grouped, key_rows, preferred_element_type=jnp.float32)
    scores = scores * head_dim ** (-0.5)
    page_index = lax.broadcasted_iota(jnp.int32, (page_count, page_len), 0)
    token_index = lax.broadcasted_iota(jnp.int32, (page_count, page_len), 1)
    position = ((page_index * tp_count + tp_index) * page_len + token_index).reshape(token_count)
    valid_mask = (position[None, :] < lengths[:, None])[:, None, None, :]
    scores = jnp.where(valid_mask, scores, NEG_BIG)
    top_score = jnp.max(scores, axis=3)
    weights = jnp.where(valid_mask, jnp.exp(scores - top_score[..., None]), 0.0)
    weight_sum = jnp.sum(weights, axis=3)
    weighted = jnp.einsum(
        "skgt,stkd->skgd",
        weights.astype(jnp.bfloat16),
        value_rows,
        preferred_element_type=jnp.float32,
    )
    return (
        weighted.reshape(slot_count, head_count * head_dim),
        top_score.reshape(slot_count, head_count),
        weight_sum.reshape(slot_count, head_count),
    )


def local(batch_sizes, seq_lens, page_table, queries, kv_pool, new_kv, out_weight):
    tp_count = lax.axis_size("tp")
    tp_index = lax.axis_index("tp")
    gathered = lax.all_gather(queries, "tp", axis=2, tiled=True)[0]
    kv_pages = kv_pool[0]
    page_ids = page_table[0]
    lengths = seq_lens[0]
    live_count = batch_sizes[0]
    slot_count, full_width = gathered.shape
    head_dim = HD
    head_count = HEADS
    slot_order = jnp.arange(slot_count, dtype=jnp.int32)

    def local_block(block_index, state):
        first_slot = block_index * SLOT_BLOCK
        query_rows = lax.dynamic_slice_in_dim(gathered, first_slot, SLOT_BLOCK, 0)
        block_ids = lax.dynamic_slice_in_dim(page_ids, first_slot, SLOT_BLOCK, 0)
        block_lengths = lax.dynamic_slice_in_dim(lengths, first_slot, SLOT_BLOCK, 0)
        block_slots = first_slot + jnp.arange(SLOT_BLOCK, dtype=jnp.int32)
        block_lengths = jnp.where(block_slots < live_count, block_lengths, 0)
        pieces = attend_slots(
            query_rows, kv_pages[block_ids], block_lengths, tp_index, tp_count, KV_HEADS
        )
        return tuple(
            (
                lax.dynamic_update_slice_in_dim(whole, piece, first_slot, 0)
                for whole, piece in zip(state, pieces)
            )
        )

    start_state = (
        jnp.zeros((slot_count, full_width), jnp.float32),
        jnp.full((slot_count, head_count), NEG_BIG, jnp.float32),
        jnp.zeros((slot_count, head_count), jnp.float32),
    )
    block_total = (live_count + SLOT_BLOCK - 1) // SLOT_BLOCK
    weighted, top_score, weight_sum = lax.fori_loop(0, block_total, local_block, start_state)
    own_heads = head_count // tp_count
    own_width = own_heads * head_dim
    shard_weighted, shard_top, shard_sum = (
        lax.all_to_all(weighted[None], "tp", split_axis=2, concat_axis=0, tiled=True),
        lax.all_to_all(top_score[None], "tp", split_axis=2, concat_axis=0, tiled=True),
        lax.all_to_all(weight_sum[None], "tp", split_axis=2, concat_axis=0, tiled=True),
    )
    part_top = jnp.max(shard_top, axis=0)
    shard_rescale = jnp.exp(shard_top - part_top[None])
    part_weighted = jnp.sum(shard_weighted * jnp.repeat(shard_rescale, head_dim, axis=-1), axis=0)
    part_sum = jnp.sum(shard_sum * shard_rescale, axis=0)
    fresh_rows = new_kv[0].astype(jnp.float32)
    kv_width = KV_HEADS * head_dim
    new_keys = fresh_rows[:, :kv_width].reshape(slot_count, KV_HEADS, head_dim)
    new_values = fresh_rows[:, kv_width:].reshape(slot_count, KV_HEADS, head_dim)
    head_ids = tp_index * own_heads + jnp.arange(own_heads, dtype=jnp.int32)
    head_map = (
        head_ids[:, None] // (head_count // KV_HEADS)
        == jnp.arange(KV_HEADS, dtype=jnp.int32)[None, :]
    ).astype(jnp.float32)
    own_keys = jnp.einsum("jk,skd->sjd", head_map, new_keys, precision=PRECISE)
    own_values = jnp.einsum("jk,skd->sjd", head_map, new_values, precision=PRECISE)
    own_queries = queries[0].astype(jnp.float32).reshape(slot_count, own_heads, head_dim)
    self_score = jnp.sum(own_queries * own_keys, axis=-1) * head_dim ** (-0.5)
    final_top = jnp.maximum(part_top, self_score)
    cache_rescale = jnp.exp(part_top - final_top)
    self_rescale = jnp.exp(self_score - final_top)
    numerator = part_weighted.reshape(slot_count, own_heads, head_dim) * cache_rescale[..., None]
    numerator = numerator + own_values * self_rescale[..., None]
    denominator = part_sum * cache_rescale + self_rescale
    attended = (numerator / denominator[..., None]).reshape(slot_count, own_width)
    attended = jnp.where((slot_order < live_count)[:, None], attended, 0.0).astype(jnp.bfloat16)
    projected = jnp.dot(
        attended,
        lax.all_gather(out_weight, "grp", axis=1, tiled=True),
        preferred_element_type=jnp.float32,
    )
    mixed = lax.psum(projected, "tp")
    return mixed[None]


def solution(mesh):
    return jax.shard_map(
        local,
        mesh=mesh,
        in_specs=(
            P("grp"),
            P("grp", None),
            P("grp", None, "tp"),
            P("grp", None, "tp"),
            P("grp", "tp", None, None),
            P("grp", None, None),
            P("tp", "grp"),
        ),
        out_specs=P("grp", None, None),
        check_vma=False,
    )
```

profile of v0, /device:TPU:0, one launch (start us, length us, event | category | flops | bytes accessed | tf_op | source)
XLA Modules:
  0.0 214.4 jit_solution(14500293375372935720)
XLA Ops:
  6.5 0.7 all-gather.2.cloned.1.call-update
  7.9 15.9 %all_gather.6 = bf16[1,16,4096]{2,1,0:T(8,128)(2,1)S(1)} all-gather(bf16[1,16,512]{2,1,0:T(8,128)(2,1)} %param.12), channel_id=1, replica_groups=mesh['grp'=4,'tp'=8] {'tp'}, dimensions={2}, use_global_device_ids=true | all-gather | bytes 147456 | tf_op jit(solution)/shard_map/all_gather | solution.py:54
  23.9 65.7 %while.14 = (s32[]{:T(128)}, f32[16,4096]{1,0:T(8,128)S(1)}, f32[16,64]{1,0:T(8,128)S(1)}, f32[16,64]{1,0:T(8,128)S(1)}, s32[]{:T(128)}, /*index=5*/s32[]{:T(128...) while((s32[]{:T(128)}, f32[16,4096]{1,0:T(8,128)S(1)}, ...), condition=%wide.region_3.4_spmd, body=%wide.region_0.3_spmd.sunk | while | flops 8685212 | bytes 7998579 | solution.py:87
  24.0 1.4 compare_select_fusion.8
  26.4 4.0 %gather_fusion = bf16[32,16,1024]{2,1,0:T(8,128)(2,1)S(1)} fusion(bf16[256,16,1024]{2,1,0:T(8,128)(2,1)} %get-tuple-element.223, s32[1024]{0:T(1024)S(1)} %pad_clamp_fusion.2), kind=kCustom, calls=%fused_computation.clone.1 | custom fusion | bytes 2097280 | tf_op jit(solution)/shard_map/while/body/gather | solution.py:72
  32.1 1.4 compare_select_fusion.8
  34.5 4.5 %gather_fusion = bf16[32,16,1024]{2,1,0:T(8,128)(2,1)S(1)} fusion(bf16[256,16,1024]{2,1,0:T(8,128)(2,1)} %get-tuple-element.223, s32[1024]{0:T(1024)S(1)} %pad_clamp_fusion.2), kind=kCustom, calls=%fused_computation.clone.1 | custom fusion | bytes 2097280 | tf_op jit(solution)/shard_map/while/body/gather | solution.py:72
  40.8 1.4 compare_select_fusion.8
  43.2 4.0 %gather_fusion = bf16[32,16,1024]{2,1,0:T(8,128)(2,1)S(1)} fusion(bf16[256,16,1024]{2,1,0:T(8,128)(2,1)} %get-tuple-element.223, s32[1024]{0:T(1024)S(1)} %pad_clamp_fusion.2), kind=kCustom, calls=%fused_computation.clone.1 | custom fusion | bytes 2097280 | tf_op jit(solution)/shard_map/while/body/gather | solution.py:72
  48.9 1.4 compare_select_fusion.8
  51.3 4.0 %gather_fusion = bf16[32,16,1024]{2,1,0:T(8,128)(2,1)S(1)} fusion(bf16[256,16,1024]{2,1,0:T(8,128)(2,1)} %get-tuple-element.223, s32[1024]{0:T(1024)S(1)} %pad_clamp_fusion.2), kind=kCustom, calls=%fused_computation.clone.1 | custom fusion | bytes 2097280 | tf_op jit(solution)/shard_map/while/body/gather | solution.py:72
  57.0 1.4 compare_select_fusion.8
  59.5 4.0 %gather_fusion = bf16[32,16,1024]{2,1,0:T(8,128)(2,1)S(1)} fusion(bf16[256,16,1024]{2,1,0:T(8,128)(2,1)} %get-tuple-element.223, s32[1024]{0:T(1024)S(1)} %pad_clamp_fusion.2), kind=kCustom, calls=%fused_computation.clone.1 | custom fusion | bytes 2097280 | tf_op jit(solution)/shard_map/while/body/gather | solution.py:72
  65.2 1.4 compare_select_fusion.8
  67.6 4.0 %gather_fusion = bf16[32,16,1024]{2,1,0:T(8,128)(2,1)S(1)} fusion(bf16[256,16,1024]{2,1,0:T(8,128)(2,1)} %get-tuple-element.223, s32[1024]{0:T(1024)S(1)} %pad_clamp_fusion.2), kind=kCustom, calls=%fused_computation.clone.1 | custom fusion | bytes 2097280 | tf_op jit(solution)/shard_map/while/body/gather | solution.py:72
  73.3 1.4 compare_select_fusion.8
  75.7 4.0 %gather_fusion = bf16[32,16,1024]{2,1,0:T(8,128)(2,1)S(1)} fusion(bf16[256,16,1024]{2,1,0:T(8,128)(2,1)} %get-tuple-element.223, s32[1024]{0:T(1024)S(1)} %pad_clamp_fusion.2), kind=kCustom, calls=%fused_computation.clone.1 | custom fusion | bytes 2097280 | tf_op jit(solution)/shard_map/while/body/gather | solution.py:72
  81.5 1.4 compare_select_fusion.8
  83.9 4.0 %gather_fusion = bf16[32,16,1024]{2,1,0:T(8,128)(2,1)S(1)} fusion(bf16[256,16,1024]{2,1,0:T(8,128)(2,1)} %get-tuple-element.223, s32[1024]{0:T(1024)S(1)} %pad_clamp_fusion.2), kind=kCustom, calls=%fused_computation.clone.1 | custom fusion | bytes 2097280 | tf_op jit(solution)/shard_map/while/body/gather | solution.py:72
  91.6 4.6 %all-to-all-start.1 = ((f32[8,1,128]{2,1,0:T(1,128)}), f32[8,1,128]{2,1,0:T(1,128)S(1)}, u32[]{:S(2)}, u32[]{:S(2)}) async-start(f32[8,1,128]{2,1,0:T(1,128)} %reshape.169), calls=%async_computation.1 | async-start | bytes 8192 | tf_op jit(solution)/shard_map/all_to_all | solution.py:92
  96.4 0.7 reduce.3
  97.9 3.9 %all-to-all-done.1 = f32[8,1,128]{2,1,0:T(1,128)S(1)} async-done(((f32[8,1,128]{2,1,0:T(1,128)}), f32[8,1,128]{2,1,0:T(1,128)S(1)}, u32[]{:S(2)}, u32[]{:S(2)}) %all-to-all-start.1) | async-done | bytes 4128 | tf_op jit(solution)/shard_map/all_to_all | solution.py:92
  101.8 3.3 %all-to-all-start.2 = ((f32[8,1,128]{2,1,0:T(1,128)}), f32[8,1,128]{2,1,0:T(1,128)S(1)}, u32[]{:S(2)}, u32[]{:S(2)}) async-start(f32[8,1,128]{2,1,0:T(1,128)} %reshape.171), calls=%async_computation.2 | async-start | bytes 8192 | tf_op jit(solution)/shard_map/all_to_all | solution.py:93
  106.0 19.3 %reduce.1 = f32[4096,16]{1,0:T(8,128)} reduce(f32[4096,1,16]{2,1,0:T(1,128)S(1)} %bitcast.84, f32[]{:T(128)} %broadcast.132), dimensions={1}, to_apply=%bitcast.54.reduce_sub_computation | reduce | bytes 524292
  125.3 3.0 %reshape.167 = f32[8,1,8192]{2,1,0:T(1,128)} reshape(f32[4096,16]{1,0:T(8,128)} %reduce.1) | data formatting | bytes 524288
  128.3 5.0 %all-to-all-start = ((f32[8,1,8192]{2,1,0:T(1,128)}), f32[8,1,8192]{2,1,0:T(1,128)S(1)}, u32[]{:S(2)}, u32[]{:S(2)}) async-start(f32[8,1,8192]{2,1,0:T(1,128)} %reshape.167), calls=%async_computation | async-start | bytes 524288 | tf_op jit(solution)/shard_map/all_to_all | solution.py:91
  135.5 7.5 %all-to-all-done = f32[8,1,8192]{2,1,0:T(1,128)S(1)} async-done(((f32[8,1,8192]{2,1,0:T(1,128)}), f32[8,1,8192]{2,1,0:T(1,128)S(1)}, u32[]{:S(2)}, u32[]{:S(2)}) %all-to-all-start) | async-done | bytes 262176 | tf_op jit(solution)/shard_map/all_to_all | solution.py:91
  143.1 1.2 reduce.2
  144.3 3.9 %reshape.168 = f32[4096,1,16]{2,1,0:T(1,128)S(1)} reshape(f32[8,8192]{1,0:T(8,128)S(1)} %reduce.2) | data formatting | bytes 524288
  149.0 3.4 %convolution_bitcast_fusion = f32[1,16,2880]{2,1,0:T(8,128)} fusion(bf16[512,2880]{0,1:T(8,128)(2,1)} %all-gather.2.cloned.1.call-done, bf16[16,512]{1,0:T(8,128)(2,1)S(1)} %reshape.153, pred[16]{0:T(512)(128)(4,1)S(1)} %iota_compare_fusion.1), kind=kOutput, calls=%fused_computation.22 | convolution fusion | flops 47194112 | bytes 3149840 | tf_op jit(solution)/shard_map/dot_general | solution.py:120
  152.4 53.6 %all-reduce.2.cloned.1.call-done = f32[1,16,2880]{2,1,0:T(8,128)} async-done(((f32[1,16,2880]{2,1,0:T(8,128)}), f32[1,16,2880]{2,1,0:T(8,128)}) %all-reduce.2.cloned.1.call-update) | async-done | bytes 184336 | tf_op jit(solution)/shard_map/psum | solution.py:125
  206.0 1.6 copy.58
  (201 shorter events, 28.2 us)
Async XLA Ops:
  6.5 142.4 %all-gather.2.cloned.1.call-start = ((), (), s32[]{:S(2)}) async-start(), calls=%async_computation.3 | async-start | bytes 3686400 | tf_op jit(solution)/shard_map/all_gather | solution.py:122
  23.9 72.3 %copy-start.1 = (bf16[1,16,1024]{2,1,0:T(8,128)(2,1)S(1)}, bf16[1,16,1024]{2,1,0:T(8,128)(2,1)}, u32[]{:S(2)}) copy-start(bf16[1,16,1024]{2,1,0:T(8,128)(2,1)} %param.14) | copy-start | bytes 98308
  23.9 72.3 %copy-start = (bf16[1,16,512]{2,1,0:T(8,128)(2,1)S(1)}, bf16[1,16,512]{2,1,0:T(8,128)(2,1)}, u32[]{:S(2)}) copy-start(bf16[1,16,512]{2,1,0:T(8,128)(2,1)} %param.12) | copy-start | bytes 49156
  91.6 10.2 %all-to-all-start.1 = ((f32[8,1,128]{2,1,0:T(1,128)}), f32[8,1,128]{2,1,0:T(1,128)S(1)}, u32[]{:S(2)}, u32[]{:S(2)}) async-start(f32[8,1,128]{2,1,0:T(1,128)} %reshape.169), calls=%async_computation.1 | async-start | bytes 8192 | tf_op jit(solution)/shard_map/all_to_all | solution.py:92
  101.8 26.5 %all-to-all-start.2 = ((f32[8,1,128]{2,1,0:T(1,128)}), f32[8,1,128]{2,1,0:T(1,128)S(1)}, u32[]{:S(2)}, u32[]{:S(2)}) async-start(f32[8,1,128]{2,1,0:T(1,128)} %reshape.171), calls=%async_computation.2 | async-start | bytes 8192 | tf_op jit(solution)/shard_map/all_to_all | solution.py:93
  128.3 14.7 %all-to-all-start = ((f32[8,1,8192]{2,1,0:T(1,128)}), f32[8,1,8192]{2,1,0:T(1,128)S(1)}, u32[]{:S(2)}, u32[]{:S(2)}) async-start(f32[8,1,8192]{2,1,0:T(1,128)} %reshape.167), calls=%async_computation | async-start | bytes 524288 | tf_op jit(solution)/shard_map/all_to_all | solution.py:91
  133.4 72.6 %all-reduce.2.cloned.1.call-start = ((), (), s32[]{:S(2)}) async-start(), calls=%async_computation.4 | async-start | bytes 376832 | tf_op jit(solution)/shard_map/psum | solution.py:125
Sparse Core Ops, SparseCore 0:
  9.2 44.9 all-gather.1
  152.5 53.4 all-reduce.1
where the time goes:
time: 216 us; the launch traced here: 214 us
  waiting for transfers between devices  65.8 us (30%)
  local copies, waits for them, and re-layouts  53.4 us (25%)
  other arithmetic  42.9 us (20%)
  blocking collectives  15.9 us (7%)
  between operations  14.3 us (7%)
  starting transfers between devices  13.2 us (6%)
  matrix products  8.29 us (4%)
    psum x1, waiting for transfers between devices, local(): mixed = lax.psum(projected, 'tp')  53.6 us
    gather x8, local copies, waits for them, and re-layouts, local_block(): kv_pages[block_ids]  32.4 us
    unnamed x3, other arithmetic  20.7 us
    all_gather x1, blocking collectives, local(): gathered = lax.all_gather(queries, 'tp', axis=2, tiled=True)[0]  15.9 us
    select_n x8, other arithmetic, local_block(): block_lengths = jnp.where(block_slots < live_count, block_lengths, 0)  11 us
    unnamed x12, local copies, waits for them, and re-layouts  10.6 us
    all_to_all x1, waiting for transfers between devices, local(): lax.all_to_all(weighted[None], 'tp', split_axis=2, concat_axis=0, tiled=T...  7.53 us
    select_n x8, other arithmetic, local_block(): kv_pages[block_ids]  5.57 us
  transfers between devices with their start and end apart: 5, of which 3 were waited for; matrix products, arithmetic and copies ran while one was open for 46% of the time, Pallas kernels for 0%

commit v1 on v0

--- a/solution.py
+++ b/solution.py
@@ -122,7 +122,9 @@
         lax.all_gather(out_weight, "grp", axis=1, tiled=True),
         preferred_element_type=jnp.float32,
     )
-    mixed = lax.psum(projected, "tp")
+    mixed = projected
+    for hop in (1, 2, 4):
+        mixed = mixed + lax.ppermute(mixed, "tp", [(dev, dev ^ hop) for dev in range(8)])
     return mixed[None]
 
 

time: 216 us -> 180 us (0.83)
  waiting for transfers between devices: 65.8 us -> 31.2 us
    psum x1 -> x0, waiting for transfers between devices: 53.6 us -> none  [local(): mixed = lax.psum(projected, 'tp')]
    ppermute x0 -> x3, waiting for transfers between devices: none -> 18.8 us  [local(): lax.ppermute(mixed, 'tp', [(dev, dev ^ hop) for dev in range(8)])]
    unnamed x12 -> x11, local copies, waits for them, and re-layouts: 10.6 us -> 9.02 us
  transfers between devices with their start and end apart: 5 -> 7, of which waited for: 3 -> 5; matrix products, arithmetic and copies ran while one was open for 46% -> 56% of each run, Pallas kernels for 0% -> 0%
where the time goes in v1:
time: 180 us; the launch traced here: 178 us
  local copies, waits for them, and re-layouts  51.8 us (29%)
  other arithmetic  43.6 us (24%)
  waiting for transfers between devices  31.2 us (17%)
  blocking collectives  15.9 us (9%)
  between operations  14.3 us (8%)
  starting transfers between devices  13.3 us (7%)
  matrix products  7.59 us (4%)
    gather x8, local copies, waits for them, and re-layouts, local_block(): kv_pages[block_ids]  32.4 us
    unnamed x3, other arithmetic  20.7 us
    ppermute x3, waiting for transfers between devices, local(): lax.ppermute(mixed, 'tp', [(dev, dev ^ hop) for dev in range(8)])  18.8 us
    all_gather x1, blocking collectives, local(): gathered = lax.all_gather(queries, 'tp', axis=2, tiled=True)[0]  15.9 us
    select_n x8, other arithmetic, local_block(): block_lengths = jnp.where(block_slots < live_count, block_lengths, 0)  11 us
    unnamed x11, local copies, waits for them, and re-layouts  9.02 us
    all_to_all x1, waiting for transfers between devices, local(): lax.all_to_all(weighted[None], 'tp', split_axis=2, concat_axis=0, tiled=T...  7.76 us
    select_n x8, other arithmetic, local_block(): kv_pages[block_ids]  5.57 us
  transfers between devices with their start and end apart: 7, of which 5 were waited for; matrix products, arithmetic and copies ran while one was open for 56% of the time, Pallas kernels for 0%

profile of v1, /device:TPU:0, one launch (start us, length us, event | category | flops | bytes accessed | tf_op | source)
XLA Modules:
  0.0 178.4 jit_solution(17001580891018461481)
XLA Ops:
  6.5 0.7 all-gather.2.cloned.1.call-update
  7.9 15.9 %all_gather.6 = bf16[1,16,4096]{2,1,0:T(8,128)(2,1)S(1)} all-gather(bf16[1,16,512]{2,1,0:T(8,128)(2,1)} %param.12), channel_id=1, replica_groups=mesh['grp'=4,'tp'=8] {'tp'}, dimensions={2}, use_global_device_ids=true | all-gather | bytes 147456 | tf_op jit(solution)/shard_map/all_gather | solution.py:54
  23.9 65.7 %while.14 = (s32[]{:T(128)}, f32[16,4096]{1,0:T(8,128)S(1)}, f32[16,64]{1,0:T(8,128)S(1)}, f32[16,64]{1,0:T(8,128)S(1)}, s32[]{:T(128)}, /*index=5*/s32[]{:T(128...) while((s32[]{:T(128)}, f32[16,4096]{1,0:T(8,128)S(1)}, ...), condition=%wide.region_3.4_spmd, body=%wide.region_0.3_spmd.sunk | while | flops 8685212 | bytes 7998579 | solution.py:87
  24.0 1.4 compare_select_fusion.8
  26.4 4.0 %gather_fusion = bf16[32,16,1024]{2,1,0:T(8,128)(2,1)S(1)} fusion(bf16[256,16,1024]{2,1,0:T(8,128)(2,1)} %get-tuple-element.223, s32[1024]{0:T(1024)S(1)} %pad_clamp_fusion.2), kind=kCustom, calls=%fused_computation.clone.1 | custom fusion | bytes 2097280 | tf_op jit(solution)/shard_map/while/body/gather | solution.py:72
  32.1 1.4 compare_select_fusion.8
  34.5 4.5 %gather_fusion = bf16[32,16,1024]{2,1,0:T(8,128)(2,1)S(1)} fusion(bf16[256,16,1024]{2,1,0:T(8,128)(2,1)} %get-tuple-element.223, s32[1024]{0:T(1024)S(1)} %pad_clamp_fusion.2), kind=kCustom, calls=%fused_computation.clone.1 | custom fusion | bytes 2097280 | tf_op jit(solution)/shard_map/while/body/gather | solution.py:72
  40.7 1.4 compare_select_fusion.8
  43.2 4.0 %gather_fusion = bf16[32,16,1024]{2,1,0:T(8,128)(2,1)S(1)} fusion(bf16[256,16,1024]{2,1,0:T(8,128)(2,1)} %get-tuple-element.223, s32[1024]{0:T(1024)S(1)} %pad_clamp_fusion.2), kind=kCustom, calls=%fused_computation.clone.1 | custom fusion | bytes 2097280 | tf_op jit(solution)/shard_map/while/body/gather | solution.py:72
  48.9 1.4 compare_select_fusion.8
  51.3 4.0 %gather_fusion = bf16[32,16,1024]{2,1,0:T(8,128)(2,1)S(1)} fusion(bf16[256,16,1024]{2,1,0:T(8,128)(2,1)} %get-tuple-element.223, s32[1024]{0:T(1024)S(1)} %pad_clamp_fusion.2), kind=kCustom, calls=%fused_computation.clone.1 | custom fusion | bytes 2097280 | tf_op jit(solution)/shard_map/while/body/gather | solution.py:72
  57.0 1.4 compare_select_fusion.8
  59.4 4.0 %gather_fusion = bf16[32,16,1024]{2,1,0:T(8,128)(2,1)S(1)} fusion(bf16[256,16,1024]{2,1,0:T(8,128)(2,1)} %get-tuple-element.223, s32[1024]{0:T(1024)S(1)} %pad_clamp_fusion.2), kind=kCustom, calls=%fused_computation.clone.1 | custom fusion | bytes 2097280 | tf_op jit(solution)/shard_map/while/body/gather | solution.py:72
  65.2 1.4 compare_select_fusion.8
  67.6 4.0 %gather_fusion = bf16[32,16,1024]{2,1,0:T(8,128)(2,1)S(1)} fusion(bf16[256,16,1024]{2,1,0:T(8,128)(2,1)} %get-tuple-element.223, s32[1024]{0:T(1024)S(1)} %pad_clamp_fusion.2), kind=kCustom, calls=%fused_computation.clone.1 | custom fusion | bytes 2097280 | tf_op jit(solution)/shard_map/while/body/gather | solution.py:72
  73.3 1.4 compare_select_fusion.8
  75.7 4.0 %gather_fusion = bf16[32,16,1024]{2,1,0:T(8,128)(2,1)S(1)} fusion(bf16[256,16,1024]{2,1,0:T(8,128)(2,1)} %get-tuple-element.223, s32[1024]{0:T(1024)S(1)} %pad_clamp_fusion.2), kind=kCustom, calls=%fused_computation.clone.1 | custom fusion | bytes 2097280 | tf_op jit(solution)/shard_map/while/body/gather | solution.py:72
  81.5 1.4 compare_select_fusion.8
  83.9 4.0 %gather_fusion = bf16[32,16,1024]{2,1,0:T(8,128)(2,1)S(1)} fusion(bf16[256,16,1024]{2,1,0:T(8,128)(2,1)} %get-tuple-element.223, s32[1024]{0:T(1024)S(1)} %pad_clamp_fusion.2), kind=kCustom, calls=%fused_computation.clone.1 | custom fusion | bytes 2097280 | tf_op jit(solution)/shard_map/while/body/gather | solution.py:72
  91.6 4.6 %all-to-all-start.1 = ((f32[8,1,128]{2,1,0:T(1,128)}), f32[8,1,128]{2,1,0:T(1,128)S(1)}, u32[]{:S(2)}, u32[]{:S(2)}) async-start(f32[8,1,128]{2,1,0:T(1,128)} %reshape.169), calls=%async_computation.1 | async-start | bytes 8192 | tf_op jit(solution)/shard_map/all_to_all | solution.py:92
  97.9 3.9 %all-to-all-done.1 = f32[8,1,128]{2,1,0:T(1,128)S(1)} async-done(((f32[8,1,128]{2,1,0:T(1,128)}), f32[8,1,128]{2,1,0:T(1,128)S(1)}, u32[]{:S(2)}, u32[]{:S(2)}) %all-to-all-start.1) | async-done | bytes 4128 | tf_op jit(solution)/shard_map/all_to_all | solution.py:92
  101.8 3.3 %all-to-all-start.2 = ((f32[8,1,128]{2,1,0:T(1,128)}), f32[8,1,128]{2,1,0:T(1,128)S(1)}, u32[]{:S(2)}, u32[]{:S(2)}) async-start(f32[8,1,128]{2,1,0:T(1,128)} %reshape.171), calls=%async_computation.2 | async-start | bytes 8192 | tf_op jit(solution)/shard_map/all_to_all | solution.py:93
  106.0 19.3 %reduce.1 = f32[4096,16]{1,0:T(8,128)} reduce(f32[4096,1,16]{2,1,0:T(1,128)S(1)} %bitcast.84, f32[]{:T(128)} %broadcast.132), dimensions={1}, to_apply=%bitcast.54.reduce_sub_computation | reduce | bytes 524292
  125.3 3.0 %reshape.167 = f32[8,1,8192]{2,1,0:T(1,128)} reshape(f32[4096,16]{1,0:T(8,128)} %reduce.1) | data formatting | bytes 524288
  128.3 5.0 %all-to-all-start = ((f32[8,1,8192]{2,1,0:T(1,128)}), f32[8,1,8192]{2,1,0:T(1,128)S(1)}, u32[]{:S(2)}, u32[]{:S(2)}) async-start(f32[8,1,8192]{2,1,0:T(1,128)} %reshape.167), calls=%async_computation | async-start | bytes 524288 | tf_op jit(solution)/shard_map/all_to_all | solution.py:91
  135.3 7.8 %all-to-all-done = f32[8,1,8192]{2,1,0:T(1,128)S(1)} async-done(((f32[8,1,8192]{2,1,0:T(1,128)}), f32[8,1,8192]{2,1,0:T(1,128)S(1)}, u32[]{:S(2)}, u32[]{:S(2)}) %all-to-all-start) | async-done | bytes 262176 | tf_op jit(solution)/shard_map/all_to_all | solution.py:91
  143.1 1.2 reduce.2
  144.3 3.9 %reshape.168 = f32[4096,1,16]{2,1,0:T(1,128)S(1)} reshape(f32[8,8192]{1,0:T(8,128)S(1)} %reduce.2) | data formatting | bytes 524288
  148.9 2.7 %fusion.15 = f32[16,2880]{1,0:T(8,128)S(1)} fusion(bf16[512,2880]{0,1:T(8,128)(2,1)} %all-gather.2.cloned.1.call-done, bf16[16,512]{1,0:T(8,128)(2,1)S(1)} %reshape.153, pred[16]{0:T(512)(128)(4,1)S(1)} %iota_compare_fusion.1), kind=kOutput, calls=%fused_computation.35 | convolution fusion | flops 47194112 | bytes 3149840 | tf_op jit(solution)/shard_map/dot_general | solution.py:120
  151.7 1.4 collective-permute-done
  153.3 6.7 %collective-permute-done.1 = f32[16,2880]{1,0:T(8,128)S(1)} collective-permute-done((f32[16,2880]{1,0:T(8,128)S(1)}, f32[16,2880]{1,0:T(8,128)S(1)}, u32[]{:S(2)}, u32[]{:S(2)}) %collective-permute-start.1) | collective-permute-done | bytes 184352 | tf_op jit(solution)/shard_map/ppermute | solution.py:127
  160.2 10.7 %collective-permute-done.2 = f32[16,2880]{1,0:T(8,128)S(1)} collective-permute-done((f32[16,2880]{1,0:T(8,128)S(1)}, f32[16,2880]{1,0:T(8,128)S(1)}, u32[]{:S(2)}, u32[]{:S(2)}) %collective-permute-start.2) | collective-permute-done | bytes 184352 | tf_op jit(solution)/shard_map/ppermute | solution.py:127
  (206 shorter events, 29.7 us)
Async XLA Ops:
  6.5 142.4 %all-gather.2.cloned.1.call-start = ((), (), s32[]{:S(2)}) async-start(), calls=%async_computation.3 | async-start | bytes 3686400 | tf_op jit(solution)/shard_map/all_gather | solution.py:122
  23.9 72.3 %copy-start.1 = (bf16[1,16,1024]{2,1,0:T(8,128)(2,1)S(1)}, bf16[1,16,1024]{2,1,0:T(8,128)(2,1)}, u32[]{:S(2)}) copy-start(bf16[1,16,1024]{2,1,0:T(8,128)(2,1)} %param.14) | copy-start | bytes 98308
  23.9 72.3 %copy-start = (bf16[1,16,512]{2,1,0:T(8,128)(2,1)S(1)}, bf16[1,16,512]{2,1,0:T(8,128)(2,1)}, u32[]{:S(2)}) copy-start(bf16[1,16,512]{2,1,0:T(8,128)(2,1)} %param.12) | copy-start | bytes 49156
  91.6 10.2 %all-to-all-start.1 = ((f32[8,1,128]{2,1,0:T(1,128)}), f32[8,1,128]{2,1,0:T(1,128)S(1)}, u32[]{:S(2)}, u32[]{:S(2)}) async-start(f32[8,1,128]{2,1,0:T(1,128)} %reshape.169), calls=%async_computation.1 | async-start | bytes 8192 | tf_op jit(solution)/shard_map/all_to_all | solution.py:92
  101.8 26.5 %all-to-all-start.2 = ((f32[8,1,128]{2,1,0:T(1,128)}), f32[8,1,128]{2,1,0:T(1,128)S(1)}, u32[]{:S(2)}, u32[]{:S(2)}) async-start(f32[8,1,128]{2,1,0:T(1,128)} %reshape.171), calls=%async_computation.2 | async-start | bytes 8192 | tf_op jit(solution)/shard_map/all_to_all | solution.py:93
  128.3 14.7 %all-to-all-start = ((f32[8,1,8192]{2,1,0:T(1,128)}), f32[8,1,8192]{2,1,0:T(1,128)S(1)}, u32[]{:S(2)}, u32[]{:S(2)}) async-start(f32[8,1,8192]{2,1,0:T(1,128)} %reshape.167), calls=%async_computation | async-start | bytes 524288 | tf_op jit(solution)/shard_map/all_to_all | solution.py:91
  151.6 1.5 collective-permute-start
  153.1 6.8 %collective-permute-start.1 = (f32[16,2880]{1,0:T(8,128)S(1)}, f32[16,2880]{1,0:T(8,128)S(1)}, u32[]{:S(2)}, u32[]{:S(2)}) collective-permute-start(f32[16,2880]{1,0:T(8,128)S(1)} %add.86), channel_id=1, source_target_pairs={{0,2},{1,3},{2,0},{3,1},{4,6},{5,7},{6,4},{7,5},{8,10},{9,11},{10,... | collective-permute-start | bytes 552968 | tf_op jit(solution)/shard_map/ppermute | solution.py:127
  160.0 10.9 %collective-permute-start.2 = (f32[16,2880]{1,0:T(8,128)S(1)}, f32[16,2880]{1,0:T(8,128)S(1)}, u32[]{:S(2)}, u32[]{:S(2)}) collective-permute-start(f32[16,2880]{1,0:T(8,128)S(1)} %add.87), channel_id=1, source_target_pairs={{0,4},{1,5},{2,6},{3,7},{4,0},{5,1},{6,2},{7,3},{8,12},{9,13},{10,... | collective-permute-start | bytes 552968 | tf_op jit(solution)/shard_map/ppermute | solution.py:127
Sparse Core Ops, SparseCore 0:
  9.2 44.9 all-gather.1
